TPU v7x, 256 devices: a whole 4x4x8 slice. The times are simulated.
256 devices in a mesh: gx: 8 (over z_hi, core), gy: 8 (over y, z_lo), gz: 4 (over x).
Axes of the slice: x: 4, y: 4, z: 8 (z_hi: 4, z_lo: 2; z = z_hi * 2 + z_lo), core: 2. Of those that a mesh axis runs over, the one named last changes fastest.
Arguments:
- pressure_prev: float32 [128, 192, 1024], P('gx', 'gy', 'gz'), may hold values from -6 to 6
- pressure_now: float32 [128, 192, 1024], P('gx', 'gy', 'gz'), may hold values from -6 to 6
- material: int32 [128, 192, 1024], P('gx', 'gy', 'gz'), may hold values from 0 to 7
- speed_table: float32 [8], replicated, may hold values from 0.05 to 0.32
- anchors: int32 [8, 8, 512], P('gx', 'gy', 'gz'), may hold values from 0 to 53496, as said below
- counts: int32 [8, 8, 4], P('gx', 'gy', 'gz'), may hold values from 64 to 128, as said below
- w_in: bfloat16 [512, 1024], replicated, may hold values from -0.25 to 0.25
- w_out: bfloat16 [1024, 512], replicated, may hold values from -0.1875 to 0.1875
Outputs:
- final_pressure: float32 [128, 192, 1024], P('gx', 'gy', 'gz')
- grad_in: float32 [512, 1024], P('gx')
- grad_out: float32 [1024, 512], P('gx')
Inputs may be any that keep to these rules, and one draw needn't show every extreme that they name: `anchors`: each entry is i * 24 * 256 + j * 256 + k with i <= 8, j <= 16, k <= 248, so every patch lies inside its brick; entries of a brick may repeat. The used slots of a brick are its first counts slots.
All inputs are finite; a program needn't handle non-finite values.
Results may differ from a plain program's by a relative error of at most 0.0017.
Values sent between devices are 32-bit elements; how exact they have to be, the bound alone decides.
A program may use at most 64 MiB of HBM per device.

v0:
```python
import jax
import jax.numpy as jnp
from jax import lax
from jax.sharding import PartitionSpec as P

STEPS = 8
PATCH = 8


def extended(x, sides, width):
    for axis, dim in sides:
        peers, length = (lax.axis_size(axis), x.shape[dim])
        up = [(i, (i + 1) % peers) for i in range(peers - 1)]
        down = [(j, i) for i, j in up]
        last = lax.slice_in_dim(x, length - width, length, axis=dim)
        first = lax.slice_in_dim(x, 0, width, axis=dim)
        before = lax.ppermute(last, axis, up)
        after = lax.ppermute(first, axis, down)
        x = jnp.concatenate([before, x, after], axis=dim)
    return x


def coefficient(material, speed_table):
    coef = jnp.zeros(material.shape, jnp.float32)
    for number in range(speed_table.shape[0]):
        coef = jnp.where(material == number, speed_table[number], coef)
    return coef


def update(prev, now, coef, padded):
    beside = padded[2:, 1:-1, 1:-1] + padded[:-2, 1:-1, 1:-1]
    beside = beside + padded[1:-1, 2:, 1:-1] + padded[1:-1, :-2, 1:-1]
    beside = beside + padded[1:-1, 1:-1, 2:] + padded[1:-1, 1:-1, :-2]
    return 2.0 * now - prev + coef * (beside - 6.0 * now)


def outer_sum(left, right):
    return lax.dot_general(
        left, right, (((0,), (0,)), ((), ())), preferred_element_type=jnp.float32
    )


def mlp_parts(inputs, targets, valid, total, w_in, w_out):
    scale = lax.rsqrt(jnp.mean(inputs * inputs, axis=-1, keepdims=True) + 1e-06)
    normed = (inputs * scale).astype(jnp.bfloat16)
    pre = jnp.dot(normed, w_in, preferred_element_type=jnp.float32)
    act = jax.nn.gelu(pre).astype(jnp.bfloat16)
    err = inputs + jnp.dot(act, w_out, preferred_element_type=jnp.float32) - targets
    dout = (2.0 * err * valid[:, None] / total).astype(jnp.bfloat16)
    dact = lax.dot_general(
        dout, w_out, (((1,), (1,)), ((), ())), preferred_element_type=jnp.float32
    )
    dpre = jax.vjp(jax.nn.gelu, pre)[1](dact)[0].astype(jnp.bfloat16)
    return (normed, act, dout, dpre)


def body(pressure_prev, pressure_now, material, speed_table, anchors, counts, w_in, w_out):
    coef = coefficient(material, speed_table)
    cells_x, cells_y, cells_z = pressure_now.shape
    prev, now = (pressure_prev, pressure_now)
    for step in range(STEPS):
        padded = extended(now, (("gx", 0), ("gy", 1), ("gz", 2)), 1)
        prev, now = (now, update(prev, now, coef, padded))
    local = anchors.reshape(-1)
    edge = jnp.arange(PATCH, dtype=jnp.int32)
    offsets = (
        edge[:, None, None] * (cells_y * cells_z)
        + edge[None, :, None] * cells_z
        + edge[None, None, :]
    ).reshape(-1)
    cell_index = local[:, None] + offsets[None, :]
    inputs = jnp.take(pressure_now.reshape(-1), cell_index, axis=0)
    targets = jnp.take(now.reshape(-1), cell_index, axis=0)
    slots = local.shape[0]
    used = counts.reshape(())
    total = lax.psum(used.astype(jnp.float32), ("gx", "gy", "gz"))
    valid = (jnp.arange(slots, dtype=jnp.int32) < used).astype(jnp.float32)
    normed, act, dout, dpre = mlp_parts(inputs, targets, valid, total, w_in, w_out)
    groups = lax.axis_size("gx")
    in_count = normed.shape[1] // groups
    out_count = act.shape[1] // groups
    full_in = outer_sum(normed, dpre)
    full_out = outer_sum(act, dout)
    summed_in, summed_out = lax.psum((full_in, full_out), ("gx", "gy", "gz"))
    position = lax.axis_index("gx")
    grad_in = lax.dynamic_slice_in_dim(summed_in, position * in_count, in_count, 0)
    grad_out = lax.dynamic_slice_in_dim(summed_out, position * out_count, out_count, 0)
    return (now, grad_in, grad_out)


def solution(mesh):
    return jax.shard_map(
        body,
        mesh=mesh,
        in_specs=(
            P("gx", "gy", "gz"),
            P("gx", "gy", "gz"),
            P("gx", "gy", "gz"),
            P(),
            P("gx", "gy", "gz"),
            P("gx", "gy", "gz"),
            P(),
            P(),
        ),
        out_specs=(P("gx", "gy", "gz"), P("gx", None), P("gx", None)),
        check_vma=False,
    )
```

profile of v0, /device:TPU:2, one launch (start us, length us, event | category | flops | bytes accessed | tf_op | source)
XLA Modules:
  0.0 1375.9 jit_solution(7897120378503387624)
XLA Ops:
  17.4 4.5 collective-permute-start.3
  36.6 5.7 fusion.70
  49.4 5.3 collective-permute-start.9
  58.4 3.9 collective-permute-start.11
  62.3 5.0 collective-permute-done.10
  69.2 5.7 fusion.62
  81.6 5.7 collective-permute-start.15
  91.0 4.0 collective-permute-start.17
  99.6 5.7 fusion.54
  106.6 6.7 collective-permute-start.19
  115.5 5.4 collective-permute-start.21
  124.5 3.9 collective-permute-start.23
  133.1 5.7 fusion.46
  140.1 7.6 collective-permute-start.25
  149.9 5.4 collective-permute-start.27
  158.9 3.9 collective-permute-start.29
  167.6 5.7 fusion.38
  174.5 7.6 collective-permute-start.31
  184.3 5.4 collective-permute-start.33
  194.0 3.9 collective-permute-start.35
  202.7 6.6 fusion.30
  210.6 7.3 collective-permute-start.37
  220.8 6.0 collective-permute-start.39
  227.1 362.7 %gather_fusion = f32[65536]{0:T(1024)S(1)} fusion(f32[98304]{0:T(1024)S(1)} %bitcast.25, s32[65536]{0:T(1024)S(1)} %broadcast_clamp_fusion), kind=kCustom, calls=%fused_computation.clone | custom fusion | bytes 786432 | tf_op jit(solution)/shard_map/jit(_take)/gather | solution.py:72
  601.6 6.5 fusion.22
  609.4 7.9 collective-permute-start.43
  619.4 4.9 collective-permute-start.45
  629.1 4.1 collective-permute-start.47
  633.2 86.1 %psum.21 = f32[]{:T(128)} all-reduce(f32[]{:T(128)S(6)} %convert_element_type.22), channel_id=1, replica_groups=mesh['gx'=8,'gy'=8,'gz'=4] {'gx','gy','gz'}, use_global_device_ids=true, to_apply=%region_1.3 | all-reduce | flops 1 | bytes 8 | tf_op jit(solution)/shard_map/psum | solution.py:76
  720.0 6.7 fusion.14
  727.0 362.7 %gather_fusion.1 = f32[65536]{0:T(1024)S(1)} fusion(f32[98304]{0:T(1024)S(1)} %bitcast.24, s32[65536]{0:T(1024)S(1)} %broadcast_clamp_fusion), kind=kCustom, calls=%fused_computation.1.clone | custom fusion | bytes 786432 | tf_op jit(solution)/shard_map/jit(_take)/gather | solution.py:73
  1095.1 270.6 %all-reduce.3.cloned.1.call-done = (f32[512,1024]{1,0:T(8,128)}, f32[1024,512]{1,0:T(8,128)}) async-done(((f32[512,1024]{1,0:T(8,128)}, f32[1024,512]{1,0:T(8,128)}), (f32[512,1024]{1,0:T(8,128)}, f32[1024,512]{1,0:T(8,128)})) %all-reduce.3.cloned.1.call-update) | async-done | bytes 4194320 | tf_op jit(solution)/shard_map/psum | solution.py:84
  (162 shorter events, 121.3 us)
Async XLA Ops:
  7.2 1358.4 %all-reduce.3.cloned.1.call-start = ((), (), s32[]{:S(2)}) async-start(), calls=%async_computation | async-start | bytes 8388608 | tf_op jit(solution)/shard_map/psum | solution.py:84
  23.6 10.2 collective-permute-start.4
  26.1 10.5 collective-permute-start.5
  56.4 10.9 collective-permute-start.10
  58.4 10.9 collective-permute-start.11
  80.3 7.0 collective-permute-start.14
  81.6 7.2 collective-permute-start.15
  89.1 8.7 collective-permute-start.16
  91.0 8.6 collective-permute-start.17
  105.3 8.0 collective-permute-start.18
  106.6 7.5 collective-permute-start.19
  122.6 8.6 collective-permute-start.22
  124.5 8.6 collective-permute-start.23
  138.8 8.9 collective-permute-start.24
  140.1 8.4 collective-permute-start.25
  157.0 8.6 collective-permute-start.28
  158.9 8.6 collective-permute-start.29
  173.2 8.9 collective-permute-start.30
  174.5 8.5 collective-permute-start.31
  192.1 8.8 collective-permute-start.34
  194.0 8.7 collective-permute-start.35
  209.3 8.8 collective-permute-start.36
  210.6 8.2 collective-permute-start.37
  219.5 370.4 %collective-permute-start.38 = (f32[18,1,256]{2,1,0:T(1,128)}, f32[18,1,256]{2,1,0:T(1,128)}, u32[]{:S(2)}, u32[]{:S(2)}) collective-permute-start(f32[18,1,256]{2,1,0:T(1,128)} %get-tuple-element.25), channel_id=1, source_target_pairs={{4,0},{8,4},{12,8},{16,12},{20,16},{24,20},{28,24},{5,1},{9,5},{13... | collective-permute-start | bytes 55304 | tf_op jit(solution)/shard_map/ppermute | solution.py:18
  220.8 369.1 %collective-permute-start.39 = (f32[18,1,256]{2,1,0:T(1,128)}, f32[18,1,256]{2,1,0:T(1,128)}, u32[]{:S(2)}, u32[]{:S(2)}) collective-permute-start(f32[18,1,256]{2,1,0:T(1,128)} %get-tuple-element.24), channel_id=1, source_target_pairs={{0,4},{4,8},{8,12},{12,16},{16,20},{20,24},{24,28},{1,5},{5,9},{9,... | collective-permute-start | bytes 55304 | tf_op jit(solution)/shard_map/ppermute | solution.py:17
  590.9 8.7 collective-permute-start.40
  593.0 8.6 collective-permute-start.41
  608.1 9.2 collective-permute-start.42
  609.4 8.8 collective-permute-start.43
  618.1 8.0 collective-permute-start.44
  627.2 92.1 %collective-permute-start.46 = (f32[18,26,1]{2,1,0:T(8,128)}, f32[18,26,1]{2,1,0:T(8,128)S(1)}, u32[]{:S(2)}, u32[]{:S(2)}) collective-permute-start(f32[18,26,1]{2,1,0:T(8,128)} %get-tuple-element.6), channel_id=1, source_target_pairs={{1,0},{2,1},{3,2},{5,4},{6,5},{7,6},{9,8},{10,9},{11,10},{13,12},{... | collective-permute-start | bytes 5624 | tf_op jit(solution)/shard_map/ppermute | solution.py:18
  629.1 90.9 %collective-permute-start.47 = (f32[18,26,1]{2,1,0:T(8,128)}, f32[18,26,1]{2,1,0:T(8,128)}, u32[]{:S(2)}, u32[]{:S(2)}) collective-permute-start(f32[18,26,1]{2,1,0:T(8,128)} %get-tuple-element.7), channel_id=1, source_target_pairs={{0,1},{1,2},{2,3},{4,5},{5,6},{6,7},{8,9},{9,10},{10,11},{12,13},{... | collective-permute-start | bytes 5624 | tf_op jit(solution)/shard_map/ppermute | solution.py:17
  (31 other events, 2823.8 us)
Sparse Core Ops, SparseCore 0:
  1095.2 270.4 all-reduce.2
where the time goes:
time: 1380 us
  local copies, waits for them, and re-layouts  735 us (53%)
  waiting for transfers between devices  325 us (24%)
  starting transfers between devices  156 us (11%)
  blocking collectives  86.1 us (6%)
  other arithmetic  50.9 us (4%)
  between operations  15.7 us (1%)
    gather x2, local copies, waits for them, and re-layouts, body(): targets = jnp.take(now.reshape(-1), cell_index, axis=0)  363 us
    gather x2, local copies, waits for them, and re-layouts, body(): inputs = jnp.take(pressure_now.reshape(-1), cell_index, axis=0)  363 us
    psum x1, waiting for transfers between devices, body(): summed_in, summed_out = lax.psum((full_in, full_out), ('gx', 'gy', 'gz'))  271 us
    ppermute x24, starting transfers between devices, extended(): before = lax.ppermute(last, axis, up)  120 us
    psum x1, blocking collectives, body(): total = lax.psum(used.astype(jnp.float32), ('gx', 'gy', 'gz'))  86.1 us
    add x8, other arithmetic, update(): return 2.0 * now - prev + coef * (beside - 6.0 * now)  48.1 us
    ppermute x24, starting transfers between devices, extended(): after = lax.ppermute(first, axis, down)  36.7 us
    ppermute x24, waiting for transfers between devices, extended(): before = lax.ppermute(last, axis, up)  28.2 us
  transfers between devices with their start and end apart: 49, of which 29 were waited for; matrix products, arithmetic and copies ran while one was open for 27% of the time, Pallas kernels for 0%

commit v1 on v0

--- a/solution.py
+++ b/solution.py
@@ -5,6 +5,11 @@
 
 STEPS = 8
 PATCH = 8
+
+
+def one_after_other(value, leading, second):
+    partial = lax.psum(value, leading)
+    return lax.psum(partial, second)
 
 
 def extended(x, sides, width):
@@ -81,7 +86,7 @@
     out_count = act.shape[1] // groups
     full_in = outer_sum(normed, dpre)
     full_out = outer_sum(act, dout)
-    summed_in, summed_out = lax.psum((full_in, full_out), ("gx", "gy", "gz"))
+    summed_in, summed_out = one_after_other((full_in, full_out), ("gy", "gz"), "gx")
     position = lax.axis_index("gx")
     grad_in = lax.dynamic_slice_in_dim(summed_in, position * in_count, in_count, 0)
     grad_out = lax.dynamic_slice_in_dim(summed_out, position * out_count, out_count, 0)

time: 1380 us -> 1550 us (1.12)
  waiting for transfers between devices: 325 us -> 500 us
    psum x1 -> x2, waiting for transfers between devices: 271 us -> 445 us  [the longest x1 326 us: one_after_other(): partial = lax.psum(value, leading)]
  transfers between devices with their start and end apart: 49 -> 50, of which waited for: 29 -> 30; matrix products, arithmetic and copies ran while one was open for 27% -> 24% of each run, Pallas kernels for 0% -> 0%
where the time goes in v1:
time: 1550 us
  local copies, waits for them, and re-layouts  735 us (47%)
  waiting for transfers between devices  500 us (32%)
  starting transfers between devices  156 us (10%)
  blocking collectives  86.1 us (6%)
  other arithmetic  49.8 us (3%)
  between operations  15.7 us (1%)
    gather x2, local copies, waits for them, and re-layouts, body(): inputs = jnp.take(pressure_now.reshape(-1), cell_index, axis=0)  363 us
    gather x2, local copies, waits for them, and re-layouts, body(): targets = jnp.take(now.reshape(-1), cell_index, axis=0)  363 us
    psum x1, waiting for transfers between devices, one_after_other(): partial = lax.psum(value, leading)  326 us
    ppermute x24, starting transfers between devices, extended(): before = lax.ppermute(last, axis, up)  120 us
    psum x1, waiting for transfers between devices, one_after_other(): return lax.psum(partial, second)  119 us
    psum x1, blocking collectives, body(): total = lax.psum(used.astype(jnp.float32), ('gx', 'gy', 'gz'))  86.1 us
    add x8, other arithmetic, update(): return 2.0 * now - prev + coef * (beside - 6.0 * now)  47 us
    ppermute x24, starting transfers between devices, extended(): after = lax.ppermute(first, axis, down)  36.7 us
  transfers between devices with their start and end apart: 50, of which 30 were waited for; matrix products, arithmetic and copies ran while one was open for 24% of the time, Pallas kernels for 0%

profile of v1, /device:TPU:2, one launch (start us, length us, event | category | flops | bytes accessed | tf_op | source)
XLA Modules:
  0.0 1549.5 jit_solution(15967348472203398156)
XLA Ops:
  17.4 4.5 collective-permute-start.3
  36.6 5.5 fusion.70
  49.2 5.3 collective-permute-start.9
  58.2 3.9 collective-permute-start.11
  62.2 5.0 collective-permute-done.10
  69.1 5.5 fusion.62
  81.4 5.7 collective-permute-start.15
  90.7 4.0 collective-permute-start.17
  99.4 5.5 fusion.54
  106.2 6.7 collective-permute-start.19
  115.1 5.4 collective-permute-start.21
  132.7 5.5 fusion.46
  139.6 7.6 collective-permute-start.25
  149.4 5.4 collective-permute-start.27
  167.0 5.5 fusion.38
  173.9 7.6 collective-permute-start.31
  183.7 5.4 collective-permute-start.33
  193.4 3.9 collective-permute-start.35
  202.1 6.5 fusion.30
  209.9 7.3 collective-permute-start.37
  220.0 6.0 collective-permute-start.39
  226.3 362.7 %gather_fusion = f32[65536]{0:T(1024)S(1)} fusion(f32[98304]{0:T(1024)S(1)} %bitcast.25, s32[65536]{0:T(1024)S(1)} %broadcast_clamp_fusion), kind=kCustom, calls=%fused_computation.clone | custom fusion | bytes 786432 | tf_op jit(solution)/shard_map/jit(_take)/gather | solution.py:77
  592.2 3.9 collective-permute-start.41
  600.8 6.3 fusion.22
  608.5 7.9 collective-permute-start.43
  618.5 4.8 collective-permute-start.45
  628.2 4.1 collective-permute-start.47
  632.3 86.1 %psum.35 = f32[]{:T(128)} all-reduce(f32[]{:T(128)S(6)} %convert_element_type.22), channel_id=1, replica_groups=mesh['gx'=8,'gy'=8,'gz'=4] {'gx','gy','gz'}, use_global_device_ids=true, to_apply=%region_1.3 | all-reduce | flops 1 | bytes 8 | tf_op jit(solution)/shard_map/psum | solution.py:81
  719.1 6.5 fusion.14
  725.9 362.7 %gather_fusion.1 = f32[65536]{0:T(1024)S(1)} fusion(f32[98304]{0:T(1024)S(1)} %bitcast.24, s32[65536]{0:T(1024)S(1)} %broadcast_clamp_fusion), kind=kCustom, calls=%fused_computation.1.clone | custom fusion | bytes 786432 | tf_op jit(solution)/shard_map/jit(_take)/gather | solution.py:78
  1094.1 326.0 %all-reduce.5.cloned.1.call-done = (f32[512,1024]{1,0:T(8,128)}, f32[1024,512]{1,0:T(8,128)}) async-done(((f32[512,1024]{1,0:T(8,128)}, f32[1024,512]{1,0:T(8,128)}), (f32[512,1024]{1,0:T(8,128)}, f32[1024,512]{1,0:T(8,128)})) %all-reduce.5.cloned.1.call-update) | async-done | bytes 4194320 | tf_op jit(solution)/shard_map/psum | solution.py:11
  1420.1 119.2 %all-reduce.7.cloned.1.call-done = (f32[512,1024]{1,0:T(8,128)}, f32[1024,512]{1,0:T(8,128)}) async-done(((f32[512,1024]{1,0:T(8,128)}, f32[1024,512]{1,0:T(8,128)}), (f32[512,1024]{1,0:T(8,128)}, f32[1024,512]{1,0:T(8,128)})) %all-reduce.7.cloned.1.call-update) | async-done | bytes 4194320 | tf_op jit(solution)/shard_map/psum | solution.py:12
  (165 shorter events, 125.2 us)
Async XLA Ops:
  7.2 1412.8 %all-reduce.5.cloned.1.call-start = ((), (), s32[]{:S(2)}) async-start(), calls=%async_computation | async-start | bytes 8388608 | tf_op jit(solution)/shard_map/psum | solution.py:11
  23.6 10.2 collective-permute-start.4
  26.1 10.5 collective-permute-start.5
  56.3 10.9 collective-permute-start.10
  58.2 10.9 collective-permute-start.11
  81.4 7.2 collective-permute-start.15
  88.8 8.7 collective-permute-start.16
  90.7 8.6 collective-permute-start.17
  104.9 8.0 collective-permute-start.18
  106.2 7.5 collective-permute-start.19
  122.2 8.6 collective-permute-start.22
  124.1 8.6 collective-permute-start.23
  138.3 8.9 collective-permute-start.24
  139.6 8.4 collective-permute-start.25
  156.5 8.6 collective-permute-start.28
  158.4 8.6 collective-permute-start.29
  172.6 8.9 collective-permute-start.30
  173.9 8.5 collective-permute-start.31
  191.4 8.8 collective-permute-start.34
  193.4 8.7 collective-permute-start.35
  208.6 8.8 collective-permute-start.36
  209.9 8.2 collective-permute-start.37
  218.7 370.4 %collective-permute-start.38 = (f32[18,1,256]{2,1,0:T(1,128)}, f32[18,1,256]{2,1,0:T(1,128)}, u32[]{:S(2)}, u32[]{:S(2)}) collective-permute-start(f32[18,1,256]{2,1,0:T(1,128)} %get-tuple-element.27), channel_id=1, source_target_pairs={{4,0},{8,4},{12,8},{16,12},{20,16},{24,20},{28,24},{5,1},{9,5},{13... | collective-permute-start | bytes 55304 | tf_op jit(solution)/shard_map/ppermute | solution.py:23
  220.0 369.1 %collective-permute-start.39 = (f32[18,1,256]{2,1,0:T(1,128)}, f32[18,1,256]{2,1,0:T(1,128)}, u32[]{:S(2)}, u32[]{:S(2)}) collective-permute-start(f32[18,1,256]{2,1,0:T(1,128)} %get-tuple-element.26), channel_id=1, source_target_pairs={{0,4},{4,8},{8,12},{12,16},{16,20},{20,24},{24,28},{1,5},{5,9},{9,... | collective-permute-start | bytes 55304 | tf_op jit(solution)/shard_map/ppermute | solution.py:22
  590.1 8.7 collective-permute-start.40
  592.2 8.6 collective-permute-start.41
  607.2 9.2 collective-permute-start.42
  608.5 8.8 collective-permute-start.43
  617.2 8.0 collective-permute-start.44
  626.3 92.1 %collective-permute-start.46 = (f32[18,26,1]{2,1,0:T(8,128)}, f32[18,26,1]{2,1,0:T(8,128)S(1)}, u32[]{:S(2)}, u32[]{:S(2)}) collective-permute-start(f32[18,26,1]{2,1,0:T(8,128)} %get-tuple-element.8), channel_id=1, source_target_pairs={{1,0},{2,1},{3,2},{5,4},{6,5},{7,6},{9,8},{10,9},{11,10},{13,12},{... | collective-permute-start | bytes 5624 | tf_op jit(solution)/shard_map/ppermute | solution.py:23
  628.2 91.0 %collective-permute-start.47 = (f32[18,26,1]{2,1,0:T(8,128)}, f32[18,26,1]{2,1,0:T(8,128)}, u32[]{:S(2)}, u32[]{:S(2)}) collective-permute-start(f32[18,26,1]{2,1,0:T(8,128)} %get-tuple-element.9), channel_id=1, source_target_pairs={{0,1},{1,2},{2,3},{4,5},{5,6},{6,7},{8,9},{9,10},{10,11},{12,13},{... | collective-permute-start | bytes 5624 | tf_op jit(solution)/shard_map/ppermute | solution.py:22
  1094.0 445.3 %all-reduce.7.cloned.1.call-start = ((), (), s32[]{:S(2)}) async-start(), calls=%async_computation.1 | async-start | bytes 8388608 | tf_op jit(solution)/shard_map/psum | solution.py:12
  (32 other events, 2829.5 us)
Sparse Core Ops, SparseCore 0:
  1094.1 325.8 all-reduce.4
  1422.8 116.5 all-reduce.6
